TPU v7x, 32 devices: a whole 2x2x4 slice. The times are simulated.
32 devices in a mesh: dx: 4 (over y, core), dy: 4 (over z), band: 2 (over x).
Axes of the slice: x: 2, y: 2, z: 4, core: 2. Of those that a mesh axis runs over, the one named last changes fastest.
Arguments:
- states: float32 [24, 32, 8, 512], P('dx', 'dy', None, 'band'), may hold values from -6 to 6
- potential: float32 [24, 32, 8], P('dx', 'dy'), may hold values from -1 to 1
Outputs:
- orthonormal: float32 [24, 32, 8, 512], P('dx', 'dy', None, 'band')
All inputs are finite; a program needn't handle non-finite values.
Results may differ from a plain program's by a relative error of at most 0.000073.
Values sent between devices are 32-bit elements; how exact they have to be, the bound alone decides.
No kernel may reach another device: no remote copies, remote signals or barrier semaphores. Data moves between devices by JAX's collectives and lax.ppermute only.
A program may use at most 64 MiB of HBM per device.

v0:
```python
import functools

import jax
import jax.numpy as jnp
from jax import lax
from jax.experimental import pallas as pl
from jax.experimental.pallas import tpu as pltpu
from jax.sharding import PartitionSpec as P


DEGREE = 3
LANES = 128
SUBLANES = 8
PANEL = 32
PART = 16
CORES = 2
PRODUCTS = 6

coeffs = (
    -5369.0 / 1800.0,
    12.0 / 7.0,
    -15.0 / 56.0,
    10.0 / 189.0,
    -1.0 / 112.0,
    2.0 / 1925.0,
    -1.0 / 16632.0,
)
WIDTH = len(coeffs) - 1
half_width = 5.0
centre_value = 7.0
VMEM = pl.BlockSpec(memory_space=pltpu.VMEM)
SMEM = pl.BlockSpec(memory_space=pltpu.SMEM)
HBM = pl.BlockSpec(memory_space=pltpu.HBM)
ROOM = pltpu.CompilerParams(vmem_limit_bytes=24 << 20)
HIGHEST = lax.Precision.HIGHEST


def dot(a, b, dims):
    return lax.dot_general(a, b, (dims, ((), ())), precision=HIGHEST, preferred_element_type=jnp.float32)


def split(value):
    high = value.astype(jnp.bfloat16)
    rest = value - high.astype(jnp.float32)
    middle = rest.astype(jnp.bfloat16)
    return high, middle, (rest - middle.astype(jnp.float32)).astype(jnp.bfloat16)


def left_parts(parts):
    high, middle, low = parts
    return [high, high, middle, middle, high, low]


def right_parts(parts):
    high, middle, low = parts
    return [high, middle, high, middle, low, high]


def outer(left, right):
    left = jnp.concatenate(left_parts(left), axis=0)
    right = jnp.concatenate(right_parts(right), axis=0)
    return lax.dot_general(left, right, (((0,), (0,)), ((), ())), preferred_element_type=jnp.float32)


def product(left, right):
    left = jnp.concatenate(left_parts(left), axis=1)
    right = jnp.concatenate(right_parts(right), axis=0)
    return lax.dot_general(left, right, (((1,), (0,)), ((), ())), preferred_element_type=jnp.float32)


def swap_groups(arrays, group):
    count = len(arrays)
    lane = lax.broadcasted_iota(jnp.int32, arrays[0].shape, 1)
    bit = 1
    while bit < count:
        upper = (lane // (group * bit)) % 2 == 1
        out = list(arrays)
        for i in range(count):
            if i & bit == 0:
                low, high = arrays[i], arrays[i | bit]
                out[i] = jnp.where(upper, pltpu.roll(high, group * bit, 1), low)
                out[i | bit] = jnp.where(upper, high, pltpu.roll(low, LANES - group * bit, 1))
        arrays = out
        bit *= 2
    return arrays


def pack_kernel(nz, states_in, potential_in, out_ref, states, potential, arrived):
    halves = range(states.shape[0])
    fetches = [
        pltpu.make_async_copy(states_in.at[:, pl.ds(LANES * half, LANES)], states.at[half], arrived.at[half])
        for half in halves
    ]
    last = pltpu.make_async_copy(potential_in, potential, arrived.at[len(fetches)])
    for fetch in [last] + fetches:
        fetch.start()
    columns = states.shape[1] // nz
    row = lax.broadcasted_iota(jnp.int32, (nz, LANES), 0)
    lane = lax.broadcasted_iota(jnp.int32, (nz, LANES), 1)
    last.wait()
    packed = jnp.zeros((potential.shape[1], LANES), jnp.float32)
    for x in range(potential.shape[0]):
        spread = jnp.where(lane == row + nz * x, 1.0, 0.0)
        packed = packed + dot(potential[x], spread, ((1,), (0,)))
    for i in range(out_ref.shape[0]):
        out_ref[i, columns:, :] = packed
    for half in halves:
        fetches[half].wait()
        arrays = [states[half, pl.ds(z, columns, stride=nz), :] for z in range(nz)]
        for g, value in enumerate(swap_groups(arrays, LANES // nz)):
            out_ref[half * nz + g, :columns, :] = value


def filter_kernel(nz, domains_y, size_x, size_y, in_ref, out_ref, field, potential):
    domains = in_ref.shape[0]
    total_x = size_x * (domains // domains_y)
    total_y = size_y * domains_y
    columns = size_x * size_y
    group = LANES // nz
    shares = out_ref.shape[0] // domains
    share = size_x // shares

    def place(i, x):
        return size_x * (i // domains_y) + x, size_y * (i % domains_y)

    def keep(which, x, rows, value):
        field[which, WIDTH + x, rows, :] = value
        if x < WIDTH:
            field[which, WIDTH + total_x + x, rows, :] = value
        if x >= total_x - WIDTH:
            field[which, WIDTH + x - total_x, rows, :] = value

    packed = in_ref[:, columns:, :].reshape(domains * size_y, LANES)
    source = lax.broadcasted_iota(jnp.int32, (LANES, LANES), 0)
    target = lax.broadcasted_iota(jnp.int32, (LANES, LANES), 1)
    shape = (LANES, LANES * size_x)
    row = lax.broadcasted_iota(jnp.int32, shape, 0)
    lane = lax.broadcasted_iota(jnp.int32, shape, 1)
    spread = jnp.where(row == nz * (lane // LANES) + lane % LANES // group, 1.0, 0.0).astype(jnp.bfloat16)
    spread_all = lax.dot_general(
        jnp.concatenate(split(packed), axis=1),
        jnp.concatenate([spread] * 3, axis=0),
        (((1,), (0,)), ((), ())),
        preferred_element_type=jnp.float32,
    )
    for x in range(size_x):
        values = spread_all[:, LANES * x : LANES * (x + 1)]
        for i in range(domains):
            at_x, at_y = place(i, x)
            rows = slice(at_y, at_y + size_y)
            potential[at_x, rows, :] = values[size_y * i : size_y * (i + 1)] - centre_value
            keep(0, at_x, rows, in_ref[i, size_y * x : size_y * (x + 1), :])

    def ring(distance, size):
        value = jnp.zeros(distance.shape, jnp.float32)
        for k in range(1, WIDTH + 1):
            for shift in (k, -k):
                value = value + jnp.where(distance == shift % size, coeffs[k], 0.0)
        return value

    along_z = ring((source // group - target // group + nz) % nz, nz)
    along_z = jnp.where((source - target) % group == 0, along_z, 0.0)
    along_z = along_z + jnp.where(source == target, 3.0 * coeffs[0], 0.0)
    along_z = jnp.concatenate(right_parts(split(along_z)), axis=0)
    shape = (total_y, PRODUCTS * total_y)
    row = lax.broadcasted_iota(jnp.int32, shape, 0)
    lane = lax.broadcasted_iota(jnp.int32, shape, 1)
    ring_y = ring((row - lane % total_y + total_y) % total_y, total_y)
    along_y = jnp.zeros(shape, jnp.float32)
    for part, value in enumerate(left_parts(split(ring_y))):
        along_y = jnp.where(lane // total_y == part, value.astype(jnp.float32), along_y)
    along_y = along_y.astype(jnp.bfloat16)

    for step in range(DEGREE):
        now, other = step % 2, (step + 1) % 2
        scale = 1.0 / half_width if step == 0 else 2.0 / half_width
        for x in range(total_x):
            value = field[now, WIDTH + x]
            parts = split(value)
            lap = lax.dot_general(
                jnp.concatenate(left_parts(parts), axis=1),
                along_z,
                (((1,), (0,)), ((), ())),
                preferred_element_type=jnp.float32,
            )
            lap = lap + lax.dot_general(
                along_y,
                jnp.concatenate(right_parts(parts), axis=0),
                (((1,), (0,)), ((), ())),
                preferred_element_type=jnp.float32,
            )
            for k in range(1, WIDTH + 1):
                lap = lap + coeffs[k] * (field[now, WIDTH + x + k] + field[now, WIDTH + x - k])
            result = (potential[x] * value - 0.5 * lap) * scale
            if step > 0:
                result = result - field[other, WIDTH + x]
            if step + 1 < DEGREE:
                keep(other, x, slice(None), result)
                continue
            for j in range(domains_y):
                i = x // size_x * domains_y + j
                row = size_y * (x % share)
                out_ref[i * shares + x % size_x // share, row : row + size_y, :] = result[size_y * j : size_y * (j + 1)]


def unpack(nz, bands, in_ref, strip):
    per_band = in_ref.shape[0] // (nz * bands)
    first = nz * (strip % per_band)
    arrays = [in_ref[(first + g) * bands + strip // per_band] for g in range(nz)]
    return swap_groups(arrays, LANES // nz)


def unpack_kernel(nz, bands, in_ref, out_ref):
    for strip in range(out_ref.shape[0]):
        for z, value in enumerate(unpack(nz, bands, in_ref, strip)):
            out_ref[strip, pl.ds(z, in_ref.shape[1], stride=nz), :] = value


def upper_blocks(strips):
    return [(i, j) for i in range(strips) for j in range(i, strips)]


def share_of(strips, core):
    return upper_blocks(strips)[core :: CORES]


def gram_kernel(nz, bands, core_ref, own_ref, other_in, out_ref, other_ref):
    strips = own_ref.shape[0]
    unpack_kernel(nz, bands, other_in, other_ref)
    parts = [split(jnp.concatenate([own_ref[strip], other_ref[strip]], axis=0)) for strip in range(strips)]
    for core in range(CORES):

        @pl.when(core_ref[0] == core)
        def _(core=core):
            pairs = share_of(strips, core)
            for left in sorted({i for i, _ in pairs}):
                spots = [at for at, (i, _) in enumerate(pairs) if i == left]
                right = [jnp.concatenate([parts[pairs[at][1]][p] for at in spots], axis=1) for p in range(3)]
                value = product([part.T for part in parts[left]], right)
                for n, at in enumerate(spots):
                    out_ref[LANES * at : LANES * (at + 1), :] = value[:, LANES * n : LANES * (n + 1)]


def sum_kernel(total, in_ref, out_ref):
    value = in_ref[0]
    for i in range(1, in_ref.shape[0]):
        value = value + in_ref[i]
    value = value / total
    for i in range(out_ref.shape[0]):
        out_ref[i] = value


def spread_row(value, row):
    return jnp.broadcast_to(value[row : row + 1, :], value.shape)


def eliminate(rows, start):
    rows = list(rows)
    tiles = len(rows)
    sublane = lax.broadcasted_iota(jnp.int32, (SUBLANES, LANES), 0)
    at = lax.broadcasted_iota(jnp.int32, (SUBLANES, LANES), 1) - start
    pivots = [jnp.ones((SUBLANES, LANES), jnp.float32) for _ in range(tiles)]
    for first in range(0, PANEL, PART):
        column = {
            (j, t): jnp.broadcast_to(rows[t][:, start + j : start + j + 1], (SUBLANES, LANES))
            for j in range(first, first + PART)
            for t in range(j // SUBLANES, tiles)
        }
        inside = (at >= first) & (at < first + PART)
        for t in range(tiles):
            rows[t] = jnp.where(inside, jnp.where(at == sublane + SUBLANES * t, 1.0, 0.0), rows[t])
        for k in range(first, first + PART):
            tile, row = k // SUBLANES, k % SUBLANES
            pivot = spread_row(column[k, tile], row)
            pivots[tile] = jnp.where(sublane == row, pivot, pivots[tile])
            over = 1.0 / pivot
            factor = {t: column[k, t] * over for t in range(tile, tiles)}
            for j in range(k + 1, first + PART):
                value = spread_row(column[k, j // SUBLANES], j % SUBLANES)
                for t in range(j // SUBLANES, tiles):
                    column[j, t] = column[j, t] - factor[t] * value
            factor[tile] = jnp.where(sublane > row, factor[tile], 0.0)
            value = spread_row(rows[tile], row)
            for t in range(tile, tiles):
                rows[t] = rows[t] - factor[t] * value
    return [rows[t] * lax.rsqrt(pivots[t]) for t in range(tiles)]


def inverse_of_block(value):
    rest = [value[t : t + SUBLANES] for t in range(0, LANES, SUBLANES)]
    lane = lax.broadcasted_iota(jnp.int32, (SUBLANES, LANES), 1)
    out = []
    for start in range(0, LANES, PANEL):
        end = start + PANEL
        rows = eliminate(rest[start // SUBLANES : end // SUBLANES], start)
        out += [jnp.where(lane < end, row, 0.0) for row in rows]
        if end < LANES:
            parts = split(jnp.concatenate(rows, axis=0))
            update = outer(parts, parts)
            for t in range(end // SUBLANES, LANES // SUBLANES):
                old = jnp.where((lane >= start) & (lane < end), 0.0, rest[t])
                rest[t] = old - update[SUBLANES * t : SUBLANES * (t + 1)]
    return jnp.concatenate(out, axis=0)


def beside(left, right):
    return tuple(jnp.concatenate(pair, axis=1) for pair in zip(left, right))


def inverse_factor(matrix, inverse):
    size = matrix.shape[0]
    for low in range(0, size, LANES):
        high = low + LANES
        rows = slice(low, high)
        block = inverse_of_block(matrix[rows, rows])
        left = split(block)
        inverse[rows, rows] = block
        if high < size:
            inverse[rows, high:] = jnp.zeros((LANES, size - high), jnp.float32)
            following = slice(high, high + LANES)
            above = split(product(left, split(matrix[rows, following])))
            matrix[following, following] = matrix[following, following] - outer(above, above)
            if high + LANES < size:
                above = beside(above, split(product(left, split(matrix[rows, high + LANES :]))))
        below = left
        if low:
            value = product(left, split(matrix[rows, :low]))
            inverse[rows, :low] = value
            below = beside(split(value), left)
        for at in range(high, size, LANES):
            mine = tuple(part[:, at - high : at - high + LANES] for part in above)
            target = slice(at, at + LANES)
            update = outer(mine, below)
            if low:
                matrix[target, :low] = matrix[target, :low] - update[:, :low]
            matrix[target, rows] = -update[:, low:]
            first = max(at, high + LANES)
            if first < size:
                update = outer(mine, tuple(part[:, first - high :] for part in above))
                matrix[target, first:] = matrix[target, first:] - update


def prepare_kernel(place_ref, own_ref, other_ref, *out_refs):
    strips, cells, _ = own_ref.shape
    band = place_ref[1]
    for strip in range(strips):
        for share, value in ((band, own_ref[strip]), (1 - band, other_ref[strip])):
            rows = pl.ds(pl.multiple_of(share * cells, cells), cells)
            for ref, part in zip(out_refs, split(value)):
                ref[strip, rows, :] = part


def finish_kernel(place_ref, mine_ref, theirs_ref, high_ref, middle_ref, low_ref, out_ref, matrix, inverse):
    strips = high_ref.shape[0]
    block = out_ref.shape[1]
    rows = mine_ref.shape[1]
    for core in range(CORES):

        @pl.when(place_ref[0] == core)
        def _(core=core):
            for ref, holder in ((mine_ref, core), (theirs_ref, 1 - core)):
                for at, (i, j) in enumerate(share_of(strips, holder)):
                    for r in range(0, LANES, SUBLANES):
                        piece, row = divmod(LANES * at + r, rows)
                        top, left = LANES * i + r, LANES * j
                        matrix[top : top + SUBLANES, left : left + LANES] = ref[piece, row : row + SUBLANES, :]

    inverse_factor(matrix, inverse)
    band = place_ref[1]
    for b in range(strips * LANES // block):

        @pl.when(band == b)
        def _(b=b):
            used = block * (b + 1)
            left = left_parts(
                [
                    jnp.concatenate([ref[s] for s in range(used // LANES)], axis=1)
                    for ref in (high_ref, middle_ref, low_ref)
                ]
            )
            right = right_parts(split(inverse[block * b : used, :used]))
            out_ref[...] = lax.dot_general(
                jnp.concatenate(left, axis=1),
                jnp.concatenate(right, axis=1),
                (((1,), (1,)), ((), ())),
                preferred_element_type=jnp.float32,
            )


def factor_kernel(in_ref, out_ref, matrix):
    matrix[...] = in_ref[...]
    inverse_factor(matrix, out_ref)


def call(kernel, shape, *args, scratch=(), scalars=0):
    specs = [SMEM] * scalars + [VMEM] * (len(args) - scalars)
    return pl.pallas_call(
        kernel,
        out_shape=jax.ShapeDtypeStruct(shape, jnp.float32),
        in_specs=specs,
        out_specs=VMEM,
        scratch_shapes=list(scratch),
        compiler_params=ROOM,
    )(*args)


def transposed(states, potential):
    size_x, size_y, nz, block = states.shape
    domains_y = lax.axis_size("dy")
    domains_x = lax.axis_size("chip") * CORES
    domains = domains_x * domains_y
    bands = lax.axis_size("band")
    cells = size_x * size_y * nz
    columns = size_x * size_y
    area = ("chip", "core", "dy")
    everyone = area + ("band",)
    same_core = ("chip", "dy", "band")
    swap = [(0, 1), (1, 0)]
    place = jnp.stack([lax.axis_index("core"), lax.axis_index("band")]).astype(jnp.int32)

    packed = pl.pallas_call(
        functools.partial(pack_kernel, nz),
        out_shape=jax.ShapeDtypeStruct((domains, columns + size_y, LANES), jnp.float32),
        in_specs=[HBM, HBM],
        out_specs=VMEM,
        scratch_shapes=[
            pltpu.VMEM((block // LANES, cells, LANES), jnp.float32),
            pltpu.VMEM(potential.shape, jnp.float32),
            pltpu.SemaphoreType.DMA((block // LANES + 1,)),
        ],
        compiler_params=ROOM,
    )(*(pltpu.with_memory_space_constraint(v, pltpu.HBM) for v in (states.reshape(cells, block), potential)))
    packed = lax.all_to_all(packed, area, 0, 0, tiled=True)
    grid = (size_x * domains_x, size_y * domains_y, LANES)
    filtered = call(
        functools.partial(filter_kernel, nz, domains_y, size_x, size_y),
        (domains * bands, columns // bands, LANES),
        packed,
        scratch=[
            pltpu.VMEM((2, grid[0] + 2 * WIDTH) + grid[1:], jnp.float32),
            pltpu.VMEM(grid, jnp.float32),
        ],
    )
    filtered = lax.all_to_all(filtered, everyone, 0, 0, tiled=True)
    size = block * bands
    strips = size // LANES
    rows = len(share_of(strips, 0)) * LANES
    holders = domains * bands // CORES
    neighbours = lax.ppermute(filtered, "core", swap)
    split_cells = (strips, cells // bands, LANES)
    own = call(functools.partial(unpack_kernel, nz, bands), split_cells, filtered)
    partial = call(
        functools.partial(gram_kernel, nz, bands),
        (rows, LANES),
        place,
        own,
        neighbours,
        scratch=[pltpu.VMEM(split_cells, jnp.float32)],
        scalars=1,
    )
    other = lax.ppermute(own, "band", swap)
    partial = lax.all_to_all(partial.reshape(holders, rows // holders, LANES), same_core, 0, 0, tiled=True)
    pieces = call(functools.partial(sum_kernel, float(cells * domains)), partial.shape, partial)
    mine = lax.all_to_all(pieces, same_core, 0, 0, tiled=True)
    theirs = lax.ppermute(mine, "core", swap)
    whole_cells = (strips, cells, LANES)
    parts = pl.pallas_call(
        prepare_kernel,
        out_shape=[jax.ShapeDtypeStruct(whole_cells, jnp.bfloat16)] * 3,
        in_specs=[SMEM] + [VMEM] * 2,
        out_specs=[VMEM] * 3,
        compiler_params=ROOM,
    )(place, own, other)
    result = call(
        finish_kernel,
        (cells, block),
        place,
        mine,
        theirs,
        *parts,
        scratch=[pltpu.VMEM((size, size), jnp.float32)] * 2,
        scalars=1,
    )
    return result.reshape(states.shape)


def with_halo(cells, axis, dim, width):
    count = lax.axis_size(axis)
    size = cells.shape[dim]
    head = lax.slice_in_dim(cells, 0, width, axis=dim)
    tail = lax.slice_in_dim(cells, size - width, size, axis=dim)
    before = lax.ppermute(tail, axis, [(i, (i + 1) % count) for i in range(count)])
    after = lax.ppermute(head, axis, [((i + 1) % count, i) for i in range(count)])
    return jnp.concatenate([before, cells, after], axis=dim)


def apply_ham(field, potential):
    padded_x = with_halo(field, "dx", 0, WIDTH)
    padded_y = with_halo(field, "dy", 1, WIDTH)
    size_x = field.shape[0]
    size_y = field.shape[1]
    lap = 3.0 * coeffs[0] * field
    for shift in range(1, WIDTH + 1):
        near = (
            padded_x[WIDTH + shift : WIDTH + shift + size_x]
            + padded_x[WIDTH - shift : WIDTH - shift + size_x]
            + padded_y[:, WIDTH + shift : WIDTH + shift + size_y]
            + padded_y[:, WIDTH - shift : WIDTH - shift + size_y]
        )
        near = near + jnp.roll(field, shift, 2) + jnp.roll(field, -shift, 2)
        lap = lap + coeffs[shift] * near
    return -0.5 * lap + potential[..., None] * field


def haloed(states, potential):
    prev = states
    cur = (apply_ham(states, potential) - centre_value * states) / half_width
    for _ in range(1, DEGREE):
        nxt = 2.0 * (apply_ham(cur, potential) - centre_value * cur) / half_width - prev
        prev, cur = (cur, nxt)
    block = cur.shape[3]
    cells = cur.shape[0] * cur.shape[1] * cur.shape[2]
    local = cur.reshape(cells, block)
    gathered = lax.all_gather(local, "band", axis=1, tiled=True)
    total = cells * lax.axis_size("dx") * lax.axis_size("dy")
    partial = jnp.dot(gathered.T, gathered, precision=HIGHEST, preferred_element_type=jnp.float32) / total
    correlation = lax.psum(partial, ("dx", "dy"))
    size = correlation.shape[0]
    if size % LANES == 0:
        inverse = call(factor_kernel, (size, size), correlation, scratch=[pltpu.VMEM((size, size), jnp.float32)])
    else:
        factor = jnp.linalg.cholesky(correlation)
        inverse = jax.scipy.linalg.solve_triangular(factor, jnp.eye(size, dtype=jnp.float32), lower=True)
    my_rows = lax.dynamic_slice_in_dim(inverse, lax.axis_index("band") * block, block, 0)
    result = jnp.dot(gathered, my_rows.T, precision=HIGHEST, preferred_element_type=jnp.float32)
    return result.reshape(cur.shape)


def solution(mesh):
    domains_x, domains_y, bands = (mesh.shape[name] for name in ("dx", "dy", "band"))
    domains = domains_x * domains_y

    def run(states, potential):
        total_x, total_y, nz, size = states.shape
        size_x, size_y, block = total_x // domains_x, total_y // domains_y, size // bands
        if (
            nz == SUBLANES
            and size_y == SUBLANES
            and nz * size_x <= LANES
            and block * nz == LANES * domains
            and block % LANES == 0
            and bands == 2
            and size_x % bands == 0
            and domains_x % CORES == 0
            and (size // LANES) * (size // LANES + 1) * LANES % (2 * domains * bands * SUBLANES) == 0
            and total_x > 2 * WIDTH
            and total_y > 2 * WIDTH
        ):
            devices = mesh.devices.reshape(domains_x // CORES, CORES, domains_y, bands)
            body, over = transposed, jax.sharding.Mesh(devices, ("chip", "core", "dy", "band"))
            x_axis = ("chip", "core")
        else:
            body, over, x_axis = haloed, mesh, "dx"
        spec = P(x_axis, "dy", None, "band")
        step = jax.shard_map(
            body, mesh=over, in_specs=(spec, P(x_axis, "dy", None)), out_specs=spec, check_vma=False
        )
        return step(states, potential)

    return run
```

profile of v0, /device:TPU:0, one launch (start us, length us, event | category | flops | bytes accessed | tf_op | source)
XLA Modules:
  0.0 94.9 jit_solution(2395554978229514678)
XLA Ops:
  0.0 1.6 %shard_map.28 = f32[16,56,128]{2,1,0:T(8,128)S(1)} custom-call(f32[384,256]{1,0:T(8,128)} %bitcast.6, f32[6,8,8]{2,1,0:T(8,128)} %potential_in.1), custom_call_target="tpu_custom_call" | custom-call | tf_op jit(solution)/shard_map/pallas_call | solution.py:421
  1.6 21.4 %all_to_all.20.in_ref = f32[16,56,128]{2,1,0:T(8,128)S(1)} all-to-all(f32[16,56,128]{2,1,0:T(8,128)S(1)} %shard_map.28), channel_id=1, replica_groups=mesh['chip'=2,'core'=2,'dy'=4,'band'=2] {'chip','core','dy'}, dimensions={0} | all-to-all | bytes 917504 | tf_op jit(solution)/shard_map/all_to_all | solution.py:433
  22.9 3.4 %shard_map.29 = f32[32,24,128]{2,1,0:T(8,128)S(1)} custom-call(f32[16,56,128]{2,1,0:T(8,128)S(1)} %all_to_all.20.in_ref), custom_call_target="tpu_custom_call" | custom-call | tf_op jit(solution)/shard_map/pallas_call | solution.py:397
  26.4 16.6 %all_to_all.21.in_ref = f32[32,24,128]{2,1,0:T(8,128)S(1)} all-to-all(f32[32,24,128]{2,1,0:T(8,128)S(1)} %shard_map.29), channel_id=1, replica_groups=mesh['chip'=2,'core'=2,'dy'=4,'band'=2] {'chip','core','dy','band'}, dimensions={0} | all-to-all | bytes 786432 | tf_op jit(solution)/shard_map/all_to_all | solution.py:444
  43.0 0.0 collective-permute-start
  43.0 0.1 pad_add_fusion.core_ref.place_ref
  43.1 0.6 shard_map.30.own_ref
  43.7 1.0 %collective-permute-done.other_in = f32[32,24,128]{2,1,0:T(8,128)S(1)} collective-permute-done((f32[32,24,128]{2,1,0:T(8,128)S(1)}, f32[32,24,128]{2,1,0:T(8,128)S(1)}, u32[]{:S(2)}, u32[]{:S(2)}) %collective-permute-start) | collective-permute-done | bytes 393248 | tf_op jit(solution)/shard_map/ppermute | solution.py:449
  44.7 1.9 %shard_map.31 = f32[640,128]{1,0:T(8,128)S(1)} custom-call(s32[2]{0:T(128)S(1)} %pad_add_fusion.core_ref.place_ref, f32[4,192,128]{2,1,0:T(8,128)S(1)} %shard_map.30.own_ref, f32[32,24,128]{2,1,0:T(8,128)S(1)} %collective-permute-done.other_in), custom_call_target="tpu_custom_call" | custom-call | tf_op jit(solution)/shard_map/pallas_call | solution.py:397
  46.6 14.9 %all_to_all.22.in_ref = f32[16,40,128]{2,1,0:T(8,128)S(1)} all-to-all(f32[16,40,128]{2,1,0:T(8,128)S(1)} %bitcast.5), channel_id=1, replica_groups=mesh['chip'=2,'core'=2,'dy'=4,'band'=2] {'chip','dy','band'}, dimensions={0} | all-to-all | bytes 655360 | tf_op jit(solution)/shard_map/all_to_all | solution.py:462
  61.5 0.8 shard_map.32
  62.3 3.5 %all-to-all-start.3 = ((f32[16,40,128]{2,1,0:T(8,128)}), f32[16,40,128]{2,1,0:T(8,128)S(1)}, u32[]{:S(2)}, u32[]{:S(2)}) async-start(f32[16,40,128]{2,1,0:T(8,128)} %shard_map.32), calls=%async_computation.3 | async-start | bytes 655360 | tf_op jit(solution)/shard_map/all_to_all | solution.py:464
  65.9 1.8 %collective-permute-start.2 = (f32[4,192,128]{2,1,0:T(8,128)S(1)}, f32[4,192,128]{2,1,0:T(8,128)S(1)}, u32[]{:S(2)}, u32[]{:S(2)}) collective-permute-start(f32[4,192,128]{2,1,0:T(8,128)S(1)} %shard_map.30.own_ref), channel_id=1, source_target_pairs={{0,1},{1,0},{2,3},{3,2},{4,5},{5,4},{6,7},{7,6},{8,9},{9,8},{10,11... | collective-permute-start | bytes 1179656 | tf_op jit(solution)/shard_map/ppermute | solution.py:461
  67.7 8.8 %all-to-all-done.3.mine_ref = f32[16,40,128]{2,1,0:T(8,128)S(1)} async-done(((f32[16,40,128]{2,1,0:T(8,128)}), f32[16,40,128]{2,1,0:T(8,128)S(1)}, u32[]{:S(2)}, u32[]{:S(2)}) %all-to-all-start.3) | async-done | bytes 327712 | tf_op jit(solution)/shard_map/all_to_all | solution.py:464
  76.5 0.0 collective-permute-start.1
  76.5 2.9 %collective-permute-done.2.other_ref = f32[4,192,128]{2,1,0:T(8,128)S(1)} collective-permute-done((f32[4,192,128]{2,1,0:T(8,128)S(1)}, f32[4,192,128]{2,1,0:T(8,128)S(1)}, u32[]{:S(2)}, u32[]{:S(2)}) %collective-permute-start.2) | collective-permute-done | bytes 393248 | tf_op jit(solution)/shard_map/ppermute | solution.py:461
  79.3 0.7 shard_map.33
  80.0 0.0 collective-permute-done.1.theirs_ref
  80.0 14.9 %shard_map.34 = f32[384,256]{1,0:T(8,128)} custom-call(s32[2]{0:T(128)S(1)} %pad_add_fusion.core_ref.place_ref, f32[16,40,128]{2,1,0:T(8,128)S(1)} %all-to-all-done.3.mine_ref, f32[16,40,128]{2,1,0:T(8,128)S(1)} %collective-permute-done.1.theirs_ref, bf16[4,384,128]{2,1,0:T(8,128)(2,1)S(1)} %get-tuple-element.8.high_ref, ...), custom_call_target="tpu_custom_call" | custom-call | tf_op jit(solution)/shard_map/pallas_call | solution.py:397
Async XLA Ops:
  43.0 1.7 %collective-permute-start = (f32[32,24,128]{2,1,0:T(8,128)S(1)}, f32[32,24,128]{2,1,0:T(8,128)S(1)}, u32[]{:S(2)}, u32[]{:S(2)}) collective-permute-start(f32[32,24,128]{2,1,0:T(8,128)S(1)} %all_to_all.21.in_ref), channel_id=1, source_target_pairs={{0,8},{8,0},{1,9},{9,1},{2,10},{10,2},{3,11},{11,3},{4,12},{12,4},... | collective-permute-start | bytes 1179656 | tf_op jit(solution)/shard_map/ppermute | solution.py:449
  62.3 14.2 %all-to-all-start.3 = ((f32[16,40,128]{2,1,0:T(8,128)}), f32[16,40,128]{2,1,0:T(8,128)S(1)}, u32[]{:S(2)}, u32[]{:S(2)}) async-start(f32[16,40,128]{2,1,0:T(8,128)} %shard_map.32), calls=%async_computation.3 | async-start | bytes 655360 | tf_op jit(solution)/shard_map/all_to_all | solution.py:464
  65.9 13.5 %collective-permute-start.2 = (f32[4,192,128]{2,1,0:T(8,128)S(1)}, f32[4,192,128]{2,1,0:T(8,128)S(1)}, u32[]{:S(2)}, u32[]{:S(2)}) collective-permute-start(f32[4,192,128]{2,1,0:T(8,128)S(1)} %shard_map.30.own_ref), channel_id=1, source_target_pairs={{0,1},{1,0},{2,3},{3,2},{4,5},{5,4},{6,7},{7,6},{8,9},{9,8},{10,11... | collective-permute-start | bytes 1179656 | tf_op jit(solution)/shard_map/ppermute | solution.py:461
  76.5 3.6 %collective-permute-start.1 = (f32[16,40,128]{2,1,0:T(8,128)S(1)}, f32[16,40,128]{2,1,0:T(8,128)S(1)}, u32[]{:S(2)}, u32[]{:S(2)}) collective-permute-start(f32[16,40,128]{2,1,0:T(8,128)S(1)} %all-to-all-done.3.mine_ref), channel_id=1, source_target_pairs={{0,8},{8,0},{1,9},{9,1},{2,10},{10,2},{3,11},{11,3},{4,12},{12,4},... | collective-permute-start | bytes 983048 | tf_op jit(solution)/shard_map/ppermute | solution.py:465
where the time goes:
time: 95.3 us; the launch traced here: 94.9 us
  blocking collectives  52.9 us (56%)
  Pallas kernels  23.8 us (25%)
  waiting for transfers between devices  12.7 us (13%)
  starting transfers between devices  5.35 us (6%)
    pallas_call x5, Pallas kernels, call(): pl.pallas_call(kernel, out_shape=jax.ShapeDtypeStruct(shape, jnp.float32)...  21.6 us
    all_to_all x1, blocking collectives, transposed(): packed = lax.all_to_all(packed, area, 0, 0, tiled=True)  21.4 us
    all_to_all x1, blocking collectives, transposed(): filtered = lax.all_to_all(filtered, everyone, 0, 0, tiled=True)  16.6 us
    all_to_all x1, blocking collectives, transposed(): lax.all_to_all(partial.reshape(holders, rows // holders, LANES), same_cor...  14.9 us
    all_to_all x1, waiting for transfers between devices, transposed(): mine = lax.all_to_all(pieces, same_core, 0, 0, tiled=True)  8.8 us
    all_to_all x1, starting transfers between devices, transposed(): mine = lax.all_to_all(pieces, same_core, 0, 0, tiled=True)  3.54 us
    ppermute x1, waiting for transfers between devices, transposed(): other = lax.ppermute(own, 'band', swap)  2.87 us
  transfers between devices with their start and end apart: 4, of which 3 were waited for; matrix products, arithmetic and copies ran while one was open for 0% of the time, Pallas kernels for 1%

commit v1 on v0

--- a/solution.py
+++ b/solution.py
@@ -15,6 +15,8 @@
 PART = 16
 CORES = 2
 PRODUCTS = 6
+TILE = SUBLANES // 2
+WHOLE, HALF, QUADRANTS = range(3)
 
 coeffs = (
     -5369.0 / 1800.0,
@@ -97,18 +99,22 @@
     columns = states.shape[1] // nz
     row = lax.broadcasted_iota(jnp.int32, (nz, LANES), 0)
     lane = lax.broadcasted_iota(jnp.int32, (nz, LANES), 1)
+    tiles = columns // TILE
     last.wait()
-    packed = jnp.zeros((potential.shape[1], LANES), jnp.float32)
-    for x in range(potential.shape[0]):
-        spread = jnp.where(lane == row + nz * x, 1.0, 0.0)
-        packed = packed + dot(potential[x], spread, ((1,), (0,)))
+    packed = jnp.zeros((TILE, LANES), jnp.float32)
+    for part in range(2):
+        wide = jnp.zeros((potential.shape[1], LANES), jnp.float32)
+        for x in range(potential.shape[0]):
+            spread = jnp.where(lane == row + nz * x + LANES // 2 * part, 1.0, 0.0)
+            wide = wide + dot(potential[x], spread, ((1,), (0,)))
+        packed = packed + wide[TILE * part : TILE * (part + 1)]
     for i in range(out_ref.shape[0]):
-        out_ref[i, columns:, :] = packed
+        out_ref[i, tiles] = packed
     for half in halves:
         fetches[half].wait()
         arrays = [states[half, pl.ds(z, columns, stride=nz), :] for z in range(nz)]
         for g, value in enumerate(swap_groups(arrays, LANES // nz)):
-            out_ref[half * nz + g, :columns, :] = value
+            out_ref[half * nz + g, :tiles] = value.reshape(tiles, TILE, LANES)
 
 
 def filter_kernel(nz, domains_y, size_x, size_y, in_ref, out_ref, field, potential):
@@ -130,13 +136,14 @@
         if x >= total_x - WIDTH:
             field[which, WIDTH + x - total_x, rows, :] = value
 
-    packed = in_ref[:, columns:, :].reshape(domains * size_y, LANES)
+    packed = in_ref[:, columns // TILE].reshape(domains * TILE, LANES)
     source = lax.broadcasted_iota(jnp.int32, (LANES, LANES), 0)
     target = lax.broadcasted_iota(jnp.int32, (LANES, LANES), 1)
-    shape = (LANES, LANES * size_x)
+    shape = (LANES, 2 * LANES * size_x)
     row = lax.broadcasted_iota(jnp.int32, shape, 0)
     lane = lax.broadcasted_iota(jnp.int32, shape, 1)
-    spread = jnp.where(row == nz * (lane // LANES) + lane % LANES // group, 1.0, 0.0).astype(jnp.bfloat16)
+    held_at = nz * (lane // LANES // 2) + LANES // 2 * (lane // LANES % 2) + lane % LANES // group
+    spread = jnp.where(row == held_at, 1.0, 0.0).astype(jnp.bfloat16)
     spread_all = lax.dot_general(
         jnp.concatenate(split(packed), axis=1),
         jnp.concatenate([spread] * 3, axis=0),
@@ -144,12 +151,13 @@
         preferred_element_type=jnp.float32,
     )
     for x in range(size_x):
-        values = spread_all[:, LANES * x : LANES * (x + 1)]
+        values = [spread_all[:, LANES * at : LANES * (at + 1)] for at in (2 * x, 2 * x + 1)]
         for i in range(domains):
             at_x, at_y = place(i, x)
             rows = slice(at_y, at_y + size_y)
-            potential[at_x, rows, :] = values[size_y * i : size_y * (i + 1)] - centre_value
-            keep(0, at_x, rows, in_ref[i, size_y * x : size_y * (x + 1), :])
+            value = jnp.concatenate([part[TILE * i : TILE * (i + 1)] for part in values], axis=0)
+            potential[at_x, rows, :] = value - centre_value
+            keep(0, at_x, rows, in_ref[i, 2 * x : 2 * x + 2].reshape(size_y, LANES))
 
     def ring(distance, size):
         value = jnp.zeros(distance.shape, jnp.float32)
@@ -224,6 +232,20 @@
     return upper_blocks(strips)[core :: CORES]
 
 
+def layout(strips, core):
+    pairs = share_of(strips, core)
+    diagonal = [i for i, j in pairs if i == j]
+    return (
+        [(WHOLE, LANES, (i, j)) for i, j in pairs if i != j]
+        + [(HALF, LANES // 2, (i, i)) for i in diagonal]
+        + [(QUADRANTS, LANES // 2, (i, j)) for i, j in zip(diagonal[::2], diagonal[1::2])]
+    )
+
+
+def rows_of(strips, core):
+    return sum(rows for _, rows, _ in layout(strips, core))
+
+
 def gram_kernel(nz, bands, core_ref, own_ref, other_in, out_ref, other_ref):
     strips = own_ref.shape[0]
     unpack_kernel(nz, bands, other_in, other_ref)
@@ -233,12 +255,23 @@
         @pl.when(core_ref[0] == core)
         def _(core=core):
             pairs = share_of(strips, core)
+            blocks = {}
             for left in sorted({i for i, _ in pairs}):
                 spots = [at for at, (i, _) in enumerate(pairs) if i == left]
                 right = [jnp.concatenate([parts[pairs[at][1]][p] for at in spots], axis=1) for p in range(3)]
                 value = product([part.T for part in parts[left]], right)
                 for n, at in enumerate(spots):
-                    out_ref[LANES * at : LANES * (at + 1), :] = value[:, LANES * n : LANES * (n + 1)]
+                    blocks[pairs[at]] = value[:, LANES * n : LANES * (n + 1)]
+            lane = lax.broadcasted_iota(jnp.int32, (LANES // 2, LANES), 1)
+            at = 0
+            for kind, rows, (i, j) in layout(strips, core):
+                if kind == QUADRANTS:
+                    first, second = blocks[i, i][LANES // 2 :], blocks[j, j][LANES // 2 :]
+                    value = jnp.where(lane < LANES // 2, pltpu.roll(first, LANES // 2, 1), second)
+                else:
+                    value = blocks[i, j][:rows]
+                out_ref[at : at + rows // TILE] = value.reshape(rows // TILE, TILE, LANES)
+                at += rows // TILE
 
 
 def sum_kernel(total, in_ref, out_ref):
@@ -353,17 +386,26 @@
 def finish_kernel(place_ref, mine_ref, theirs_ref, high_ref, middle_ref, low_ref, out_ref, matrix, inverse):
     strips = high_ref.shape[0]
     block = out_ref.shape[1]
-    rows = mine_ref.shape[1]
+    held = mine_ref.shape[1]
     for core in range(CORES):
 
         @pl.when(place_ref[0] == core)
         def _(core=core):
             for ref, holder in ((mine_ref, core), (theirs_ref, 1 - core)):
-                for at, (i, j) in enumerate(share_of(strips, holder)):
-                    for r in range(0, LANES, SUBLANES):
-                        piece, row = divmod(LANES * at + r, rows)
-                        top, left = LANES * i + r, LANES * j
-                        matrix[top : top + SUBLANES, left : left + LANES] = ref[piece, row : row + SUBLANES, :]
+                tile = 0
+                for kind, rows, (i, j) in layout(strips, holder):
+                    for row in range(0, rows, SUBLANES):
+                        value = jnp.concatenate([ref[t // held, t % held] for t in (tile, tile + 1)], axis=0)
+                        tile += 2
+                        targets = [(LANES * i + row, LANES * j, value)]
+                        if kind == QUADRANTS:
+                            row += LANES // 2
+                            targets = [
+                                (LANES * i + row, LANES * i, pltpu.roll(value, LANES // 2, 1)),
+                                (LANES * j + row, LANES * j, value),
+                            ]
+                        for top, left, part in targets:
+                            matrix[top : top + SUBLANES, left : left + LANES] = part
 
     inverse_factor(matrix, inverse)
     band = place_ref[1]
@@ -420,7 +462,7 @@
 
     packed = pl.pallas_call(
         functools.partial(pack_kernel, nz),
-        out_shape=jax.ShapeDtypeStruct((domains, columns + size_y, LANES), jnp.float32),
+        out_shape=jax.ShapeDtypeStruct((domains, columns // TILE + 1, TILE, LANES), jnp.float32),
         in_specs=[HBM, HBM],
         out_specs=VMEM,
         scratch_shapes=[
@@ -444,14 +486,14 @@
     filtered = lax.all_to_all(filtered, everyone, 0, 0, tiled=True)
     size = block * bands
     strips = size // LANES
-    rows = len(share_of(strips, 0)) * LANES
+    rows = rows_of(strips, 0)
     holders = domains * bands // CORES
     neighbours = lax.ppermute(filtered, "core", swap)
     split_cells = (strips, cells // bands, LANES)
     own = call(functools.partial(unpack_kernel, nz, bands), split_cells, filtered)
     partial = call(
         functools.partial(gram_kernel, nz, bands),
-        (rows, LANES),
+        (rows // TILE, TILE, LANES),
         place,
         own,
         neighbours,
@@ -459,7 +501,7 @@
         scalars=1,
     )
     other = lax.ppermute(own, "band", swap)
-    partial = lax.all_to_all(partial.reshape(holders, rows // holders, LANES), same_core, 0, 0, tiled=True)
+    partial = lax.all_to_all(partial.reshape(holders, rows // holders // TILE, TILE, LANES), same_core, 0, 0, tiled=True)
     pieces = call(functools.partial(sum_kernel, float(cells * domains)), partial.shape, partial)
     mine = lax.all_to_all(pieces, same_core, 0, 0, tiled=True)
     theirs = lax.ppermute(mine, "core", swap)
@@ -536,6 +578,12 @@
     return result.reshape(cur.shape)
 
 
+def fits_cores(strips, devices):
+    rows = {rows_of(strips, core) for core in range(CORES)}
+    even = all(sum(i == j for i, j in share_of(strips, core)) % 2 == 0 for core in range(CORES))
+    return even and len(rows) == 1 and rows.pop() % (devices // CORES * TILE) == 0
+
+
 def solution(mesh):
     domains_x, domains_y, bands = (mesh.shape[name] for name in ("dx", "dy", "band"))
     domains = domains_x * domains_y
@@ -546,13 +594,13 @@
         if (
             nz == SUBLANES
             and size_y == SUBLANES
-            and nz * size_x <= LANES
+            and 2 * nz * size_x <= LANES
             and block * nz == LANES * domains
             and block % LANES == 0
             and bands == 2
             and size_x % bands == 0
             and domains_x % CORES == 0
-            and (size // LANES) * (size // LANES + 1) * LANES % (2 * domains * bands * SUBLANES) == 0
+            and fits_cores(size // LANES, domains * bands)
             and total_x > 2 * WIDTH
             and total_y > 2 * WIDTH
         ):

time: 95.3 us -> 93.8 us (0.984)
  blocking collectives: 52.9 us -> 51.6 us
where the time goes in v1:
time: 93.8 us; the launch traced here: 93.5 us
  blocking collectives  51.6 us (55%)
  Pallas kernels  24.1 us (26%)
  waiting for transfers between devices  12.4 us (13%)
  starting transfers between devices  5.35 us (6%)
    pallas_call x5, Pallas kernels, call(): pl.pallas_call(kernel, out_shape=jax.ShapeDtypeStruct(shape, jnp.float32)...  21.7 us
    all_to_all x1, blocking collectives, transposed(): packed = lax.all_to_all(packed, area, 0, 0, tiled=True)  20.7 us
    all_to_all x1, blocking collectives, transposed(): filtered = lax.all_to_all(filtered, everyone, 0, 0, tiled=True)  16.6 us
    all_to_all x1, blocking collectives, transposed(): lax.all_to_all(partial.reshape(holders, rows // holders // TILE, TILE, LA...  14.3 us
    all_to_all x1, waiting for transfers between devices, transposed(): mine = lax.all_to_all(pieces, same_core, 0, 0, tiled=True)  8.17 us
    all_to_all x1, starting transfers between devices, transposed(): mine = lax.all_to_all(pieces, same_core, 0, 0, tiled=True)  3.54 us
    ppermute x1, waiting for transfers between devices, transposed(): other = lax.ppermute(own, 'band', swap)  3.15 us
  transfers between devices with their start and end apart: 4, of which 3 were waited for; matrix products, arithmetic and copies ran while one was open for 0% of the time, Pallas kernels for 1%

profile of v1, /device:TPU:0, one launch (start us, length us, event | category | flops | bytes accessed | tf_op | source)
XLA Modules:
  0.0 93.5 jit_solution(6494584399259954942)
XLA Ops:
  0.0 1.7 %shard_map.28 = f32[16,13,4,128]{3,2,1,0:T(4,128)S(1)} custom-call(f32[384,256]{1,0:T(8,128)} %bitcast.6, f32[6,8,8]{2,1,0:T(8,128)} %potential_in.1), custom_call_target="tpu_custom_call" | custom-call | tf_op jit(solution)/shard_map/pallas_call | solution.py:463
  1.7 20.7 %all_to_all.20.in_ref = f32[16,13,4,128]{3,2,1,0:T(4,128)S(1)} all-to-all(f32[16,13,4,128]{3,2,1,0:T(4,128)S(1)} %shard_map.28), channel_id=1, replica_groups=mesh['chip'=2,'core'=2,'dy'=4,'band'=2] {'chip','core','dy'}, dimensions={0} | all-to-all | bytes 851968 | tf_op jit(solution)/shard_map/all_to_all | solution.py:475
  22.3 3.5 %shard_map.29 = f32[32,24,128]{2,1,0:T(8,128)S(1)} custom-call(f32[16,13,4,128]{3,2,1,0:T(4,128)S(1)} %all_to_all.20.in_ref), custom_call_target="tpu_custom_call" | custom-call | tf_op jit(solution)/shard_map/pallas_call | solution.py:439
  25.8 16.6 %all_to_all.21.in_ref = f32[32,24,128]{2,1,0:T(8,128)S(1)} all-to-all(f32[32,24,128]{2,1,0:T(8,128)S(1)} %shard_map.29), channel_id=1, replica_groups=mesh['chip'=2,'core'=2,'dy'=4,'band'=2] {'chip','core','dy','band'}, dimensions={0} | all-to-all | bytes 786432 | tf_op jit(solution)/shard_map/all_to_all | solution.py:486
  42.4 0.0 collective-permute-start
  42.4 0.1 pad_add_fusion.core_ref.place_ref
  42.5 0.6 shard_map.30.own_ref
  43.1 1.0 %collective-permute-done.other_in = f32[32,24,128]{2,1,0:T(8,128)S(1)} collective-permute-done((f32[32,24,128]{2,1,0:T(8,128)S(1)}, f32[32,24,128]{2,1,0:T(8,128)S(1)}, u32[]{:S(2)}, u32[]{:S(2)}) %collective-permute-start) | collective-permute-done | bytes 393248 | tf_op jit(solution)/shard_map/ppermute | solution.py:491
  44.1 1.9 %shard_map.31 = f32[144,4,128]{2,1,0:T(4,128)S(1)} custom-call(s32[2]{0:T(128)S(1)} %pad_add_fusion.core_ref.place_ref, f32[4,192,128]{2,1,0:T(8,128)S(1)} %shard_map.30.own_ref, f32[32,24,128]{2,1,0:T(8,128)S(1)} %collective-permute-done.other_in), custom_call_target="tpu_custom_call" | custom-call | tf_op jit(solution)/shard_map/pallas_call | solution.py:439
  46.0 14.3 %all_to_all.22.in_ref = f32[16,9,4,128]{3,2,1,0:T(4,128)S(1)} all-to-all(f32[16,9,4,128]{3,2,1,0:T(4,128)S(1)} %bitcast.5), channel_id=1, replica_groups=mesh['chip'=2,'core'=2,'dy'=4,'band'=2] {'chip','dy','band'}, dimensions={0} | all-to-all | bytes 589824 | tf_op jit(solution)/shard_map/all_to_all | solution.py:504
  60.3 0.8 shard_map.32
  61.1 3.5 %all-to-all-start.3 = ((f32[16,9,4,128]{3,2,1,0:T(4,128)}), f32[16,9,4,128]{3,2,1,0:T(4,128)S(1)}, u32[]{:S(2)}, u32[]{:S(2)}) async-start(f32[16,9,4,128]{3,2,1,0:T(4,128)} %shard_map.32), calls=%async_computation.3 | async-start | bytes 589824 | tf_op jit(solution)/shard_map/all_to_all | solution.py:506
  64.6 1.8 %collective-permute-start.2 = (f32[4,192,128]{2,1,0:T(8,128)S(1)}, f32[4,192,128]{2,1,0:T(8,128)S(1)}, u32[]{:S(2)}, u32[]{:S(2)}) collective-permute-start(f32[4,192,128]{2,1,0:T(8,128)S(1)} %shard_map.30.own_ref), channel_id=1, source_target_pairs={{0,1},{1,0},{2,3},{3,2},{4,5},{5,4},{6,7},{7,6},{8,9},{9,8},{10,11... | collective-permute-start | bytes 1179656 | tf_op jit(solution)/shard_map/ppermute | solution.py:503
  66.5 8.2 %all-to-all-done.3.mine_ref = f32[16,9,4,128]{3,2,1,0:T(4,128)S(1)} async-done(((f32[16,9,4,128]{3,2,1,0:T(4,128)}), f32[16,9,4,128]{3,2,1,0:T(4,128)S(1)}, u32[]{:S(2)}, u32[]{:S(2)}) %all-to-all-start.3) | async-done | bytes 294944 | tf_op jit(solution)/shard_map/all_to_all | solution.py:506
  74.6 0.0 collective-permute-start.1
  74.6 3.2 %collective-permute-done.2.other_ref = f32[4,192,128]{2,1,0:T(8,128)S(1)} collective-permute-done((f32[4,192,128]{2,1,0:T(8,128)S(1)}, f32[4,192,128]{2,1,0:T(8,128)S(1)}, u32[]{:S(2)}, u32[]{:S(2)}) %collective-permute-start.2) | collective-permute-done | bytes 393248 | tf_op jit(solution)/shard_map/ppermute | solution.py:503
  77.8 0.7 shard_map.33
  78.5 0.0 collective-permute-done.1.theirs_ref
  78.5 15.0 %shard_map.34 = f32[384,256]{1,0:T(8,128)} custom-call(s32[2]{0:T(128)S(1)} %pad_add_fusion.core_ref.place_ref, f32[16,9,4,128]{3,2,1,0:T(4,128)S(1)} %all-to-all-done.3.mine_ref, f32[16,9,4,128]{3,2,1,0:T(4,128)S(1)} %collective-permute-done.1.theirs_ref, bf16[4,384,128]{2,1,0:T(8,128)(2,1)S(1)} %get-tuple-element.8.high_ref, ...), custom_call_target="tpu_custom_call" | custom-call | tf_op jit(solution)/shard_map/pallas_call | solution.py:439
Async XLA Ops:
  42.4 1.7 %collective-permute-start = (f32[32,24,128]{2,1,0:T(8,128)S(1)}, f32[32,24,128]{2,1,0:T(8,128)S(1)}, u32[]{:S(2)}, u32[]{:S(2)}) collective-permute-start(f32[32,24,128]{2,1,0:T(8,128)S(1)} %all_to_all.21.in_ref), channel_id=1, source_target_pairs={{0,8},{8,0},{1,9},{9,1},{2,10},{10,2},{3,11},{11,3},{4,12},{12,4},... | collective-permute-start | bytes 1179656 | tf_op jit(solution)/shard_map/ppermute | solution.py:491
  61.1 13.5 %all-to-all-start.3 = ((f32[16,9,4,128]{3,2,1,0:T(4,128)}), f32[16,9,4,128]{3,2,1,0:T(4,128)S(1)}, u32[]{:S(2)}, u32[]{:S(2)}) async-start(f32[16,9,4,128]{3,2,1,0:T(4,128)} %shard_map.32), calls=%async_computation.3 | async-start | bytes 589824 | tf_op jit(solution)/shard_map/all_to_all | solution.py:506
  64.6 13.1 %collective-permute-start.2 = (f32[4,192,128]{2,1,0:T(8,128)S(1)}, f32[4,192,128]{2,1,0:T(8,128)S(1)}, u32[]{:S(2)}, u32[]{:S(2)}) collective-permute-start(f32[4,192,128]{2,1,0:T(8,128)S(1)} %shard_map.30.own_ref), channel_id=1, source_target_pairs={{0,1},{1,0},{2,3},{3,2},{4,5},{5,4},{6,7},{7,6},{8,9},{9,8},{10,11... | collective-permute-start | bytes 1179656 | tf_op jit(solution)/shard_map/ppermute | solution.py:503
  74.6 3.9 %collective-permute-start.1 = (f32[16,9,4,128]{3,2,1,0:T(4,128)S(1)}, f32[16,9,4,128]{3,2,1,0:T(4,128)S(1)}, u32[]{:S(2)}, u32[]{:S(2)}) collective-permute-start(f32[16,9,4,128]{3,2,1,0:T(4,128)S(1)} %all-to-all-done.3.mine_ref), channel_id=1, source_target_pairs={{0,8},{8,0},{1,9},{9,1},{2,10},{10,2},{3,11},{11,3},{4,12},{12,4},... | collective-permute-start | bytes 884744 | tf_op jit(solution)/shard_map/ppermute | solution.py:507

commit v2 on v1

--- a/solution.py
+++ b/solution.py
@@ -246,22 +246,39 @@
     return sum(rows for _, rows, _ in layout(strips, core))
 
 
-def gram_kernel(nz, bands, core_ref, own_ref, other_in, out_ref, other_ref):
-    strips = own_ref.shape[0]
-    unpack_kernel(nz, bands, other_in, other_ref)
-    parts = [split(jnp.concatenate([own_ref[strip], other_ref[strip]], axis=0)) for strip in range(strips)]
+def products(cells_ref, core):
+    strips = cells_ref.shape[0]
+    pairs = share_of(strips, core)
+    used = sorted({strip for pair in pairs for strip in pair})
+    parts = {strip: split(cells_ref[strip]) for strip in used}
+    blocks = {}
+    for left in sorted({i for i, _ in pairs}):
+        rights = [j for i, j in pairs if i == left]
+        value = product([part.T for part in parts[left]], [jnp.concatenate([parts[j][p] for j in rights], axis=1) for p in range(3)])
+        for n, j in enumerate(rights):
+            blocks[left, j] = value[:, LANES * n : LANES * (n + 1)]
+    return blocks
+
+
+def own_kernel(nz, bands, core_ref, in_ref, cells_ref, blocks_ref):
+    unpack_kernel(nz, bands, in_ref, cells_ref)
     for core in range(CORES):
 
         @pl.when(core_ref[0] == core)
         def _(core=core):
-            pairs = share_of(strips, core)
-            blocks = {}
-            for left in sorted({i for i, _ in pairs}):
-                spots = [at for at, (i, _) in enumerate(pairs) if i == left]
-                right = [jnp.concatenate([parts[pairs[at][1]][p] for at in spots], axis=1) for p in range(3)]
-                value = product([part.T for part in parts[left]], right)
-                for n, at in enumerate(spots):
-                    blocks[pairs[at]] = value[:, LANES * n : LANES * (n + 1)]
+            for at, value in enumerate(products(cells_ref, core).values()):
+                blocks_ref[at] = value
+
+
+def gram_kernel(nz, bands, core_ref, blocks_ref, in_ref, out_ref, cells_ref):
+    strips = cells_ref.shape[0]
+    unpack_kernel(nz, bands, in_ref, cells_ref)
+    for core in range(CORES):
+
+        @pl.when(core_ref[0] == core)
+        def _(core=core):
+            added = products(cells_ref, core)
+            blocks = {pair: value + blocks_ref[at] for at, (pair, value) in enumerate(added.items())}
             lane = lax.broadcasted_iota(jnp.int32, (LANES // 2, LANES), 1)
             at = 0
             for kind, rows, (i, j) in layout(strips, core):
@@ -490,12 +507,21 @@
     holders = domains * bands // CORES
     neighbours = lax.ppermute(filtered, "core", swap)
     split_cells = (strips, cells // bands, LANES)
-    own = call(functools.partial(unpack_kernel, nz, bands), split_cells, filtered)
+    own, blocks = pl.pallas_call(
+        functools.partial(own_kernel, nz, bands),
+        out_shape=[
+            jax.ShapeDtypeStruct(split_cells, jnp.float32),
+            jax.ShapeDtypeStruct((len(share_of(strips, 0)), LANES, LANES), jnp.float32),
+        ],
+        in_specs=[SMEM, VMEM],
+        out_specs=[VMEM, VMEM],
+        compiler_params=ROOM,
+    )(place, filtered)
     partial = call(
         functools.partial(gram_kernel, nz, bands),
         (rows // TILE, TILE, LANES),
         place,
-        own,
+        blocks,
         neighbours,
         scratch=[pltpu.VMEM(split_cells, jnp.float32)],
         scalars=1,

time: 93.8 us -> 94.6 us (level)
  Pallas kernels: 24.1 us -> 25.1 us
    pallas_call x0 -> x1, Pallas kernels: none -> 1.78 us  [transposed(): pl.pallas_call(functools.partial(own_kernel, nz, bands), out_shape=[jax.S...]
    ppermute x1, waiting for transfers between devices: 1.03 us -> 0.01 us  [transposed(): neighbours = lax.ppermute(filtered, 'core', swap)]
    pallas_call x5 -> x4, Pallas kernels: 21.7 us -> 21 us  [call(): pl.pallas_call(kernel, out_shape=jax.ShapeDtypeStruct(shape, jnp.float32)...]
  transfers between devices with their start and end apart: 4 -> 4, of which waited for: 3 -> 2; matrix products, arithmetic and copies ran while one was open for 0% -> 0% of each run, Pallas kernels for 1% -> 3%
where the time goes in v2:
time: 94.6 us; the launch traced here: 94.3 us
  blocking collectives  52 us (55%)
  Pallas kernels  25.1 us (27%)
  waiting for transfers between devices  11.7 us (12%)
  starting transfers between devices  5.35 us (6%)
    pallas_call x4, Pallas kernels, call(): pl.pallas_call(kernel, out_shape=jax.ShapeDtypeStruct(shape, jnp.float32)...  21 us
    all_to_all x1, blocking collectives, transposed(): packed = lax.all_to_all(packed, area, 0, 0, tiled=True)  20.7 us
    all_to_all x1, blocking collectives, transposed(): filtered = lax.all_to_all(filtered, everyone, 0, 0, tiled=True)  16.6 us
    all_to_all x1, blocking collectives, transposed(): lax.all_to_all(partial.reshape(holders, rows // holders // TILE, TILE, LA...  14.7 us
    all_to_all x1, waiting for transfers between devices, transposed(): mine = lax.all_to_all(pieces, same_core, 0, 0, tiled=True)  8.52 us
    all_to_all x1, starting transfers between devices, transposed(): mine = lax.all_to_all(pieces, same_core, 0, 0, tiled=True)  3.54 us
    ppermute x1, waiting for transfers between devices, transposed(): other = lax.ppermute(own, 'band', swap)  3.15 us
  transfers between devices with their start and end apart: 4, of which 2 were waited for; matrix products, arithmetic and copies ran while one was open for 0% of the time, Pallas kernels for 3%

profile of v2, /device:TPU:0, one launch (start us, length us, event | category | flops | bytes accessed | tf_op | source)
XLA Modules:
  0.0 94.3 jit_solution(11806915056004059662)
XLA Ops:
  0.0 1.7 %shard_map.28 = f32[16,13,4,128]{3,2,1,0:T(4,128)S(1)} custom-call(f32[384,256]{1,0:T(8,128)} %bitcast.6, f32[6,8,8]{2,1,0:T(8,128)} %potential_in.1), custom_call_target="tpu_custom_call" | custom-call | tf_op jit(solution)/shard_map/pallas_call | solution.py:480
  1.7 20.7 %all_to_all.20.in_ref = f32[16,13,4,128]{3,2,1,0:T(4,128)S(1)} all-to-all(f32[16,13,4,128]{3,2,1,0:T(4,128)S(1)} %shard_map.28), channel_id=1, replica_groups=mesh['chip'=2,'core'=2,'dy'=4,'band'=2] {'chip','core','dy'}, dimensions={0} | all-to-all | bytes 851968 | tf_op jit(solution)/shard_map/all_to_all | solution.py:492
  22.3 3.5 %shard_map.29 = f32[32,24,128]{2,1,0:T(8,128)S(1)} custom-call(f32[16,13,4,128]{3,2,1,0:T(4,128)S(1)} %all_to_all.20.in_ref), custom_call_target="tpu_custom_call" | custom-call | tf_op jit(solution)/shard_map/pallas_call | solution.py:456
  25.8 16.6 %all_to_all.21.in_ref = f32[32,24,128]{2,1,0:T(8,128)S(1)} all-to-all(f32[32,24,128]{2,1,0:T(8,128)S(1)} %shard_map.29), channel_id=1, replica_groups=mesh['chip'=2,'core'=2,'dy'=4,'band'=2] {'chip','core','dy','band'}, dimensions={0} | all-to-all | bytes 786432 | tf_op jit(solution)/shard_map/all_to_all | solution.py:503
  42.4 0.0 collective-permute-start
  42.4 0.1 pad_add_fusion.core_ref.place_ref
  42.5 1.8 %shard_map.30 = (f32[4,192,128]{2,1,0:T(8,128)S(1)}, f32[5,128,128]{2,1,0:T(8,128)S(1)}) custom-call(s32[2]{0:T(128)S(1)} %pad_add_fusion.core_ref.place_ref, f32[32,24,128]{2,1,0:T(8,128)S(1)} %all_to_all.21.in_ref), custom_call_target="tpu_custom_call" | custom-call | tf_op jit(solution)/shard_map/pallas_call | solution.py:510
  44.3 0.0 collective-permute-done.in_ref
  44.3 1.8 %shard_map.31 = f32[144,4,128]{2,1,0:T(4,128)S(1)} custom-call(s32[2]{0:T(128)S(1)} %pad_add_fusion.core_ref.place_ref, f32[5,128,128]{2,1,0:T(8,128)S(1)} %get-tuple-element.10.blocks_ref, f32[32,24,128]{2,1,0:T(8,128)S(1)} %collective-permute-done.in_ref), custom_call_target="tpu_custom_call" | custom-call | tf_op jit(solution)/shard_map/pallas_call | solution.py:456
  46.1 14.7 %all_to_all.22.in_ref = f32[16,9,4,128]{3,2,1,0:T(4,128)S(1)} all-to-all(f32[16,9,4,128]{3,2,1,0:T(4,128)S(1)} %bitcast.5), channel_id=1, replica_groups=mesh['chip'=2,'core'=2,'dy'=4,'band'=2] {'chip','dy','band'}, dimensions={0} | all-to-all | bytes 589824 | tf_op jit(solution)/shard_map/all_to_all | solution.py:530
  60.8 0.8 shard_map.32
  61.6 3.5 %all-to-all-start.3 = ((f32[16,9,4,128]{3,2,1,0:T(4,128)}), f32[16,9,4,128]{3,2,1,0:T(4,128)S(1)}, u32[]{:S(2)}, u32[]{:S(2)}) async-start(f32[16,9,4,128]{3,2,1,0:T(4,128)} %shard_map.32), calls=%async_computation.3 | async-start | bytes 589824 | tf_op jit(solution)/shard_map/all_to_all | solution.py:532
  65.1 1.8 %collective-permute-start.2 = (f32[4,192,128]{2,1,0:T(8,128)S(1)}, f32[4,192,128]{2,1,0:T(8,128)S(1)}, u32[]{:S(2)}, u32[]{:S(2)}) collective-permute-start(f32[4,192,128]{2,1,0:T(8,128)S(1)} %get-tuple-element.11.own_ref), channel_id=1, source_target_pairs={{0,1},{1,0},{2,3},{3,2},{4,5},{5,4},{6,7},{7,6},{8,9},{9,8},{10,11... | collective-permute-start | bytes 1179656 | tf_op jit(solution)/shard_map/ppermute | solution.py:529
  66.9 8.5 %all-to-all-done.3.mine_ref = f32[16,9,4,128]{3,2,1,0:T(4,128)S(1)} async-done(((f32[16,9,4,128]{3,2,1,0:T(4,128)}), f32[16,9,4,128]{3,2,1,0:T(4,128)S(1)}, u32[]{:S(2)}, u32[]{:S(2)}) %all-to-all-start.3) | async-done | bytes 294944 | tf_op jit(solution)/shard_map/all_to_all | solution.py:532
  75.5 0.0 collective-permute-start.1
  75.5 3.2 %collective-permute-done.2.other_ref = f32[4,192,128]{2,1,0:T(8,128)S(1)} collective-permute-done((f32[4,192,128]{2,1,0:T(8,128)S(1)}, f32[4,192,128]{2,1,0:T(8,128)S(1)}, u32[]{:S(2)}, u32[]{:S(2)}) %collective-permute-start.2) | collective-permute-done | bytes 393248 | tf_op jit(solution)/shard_map/ppermute | solution.py:529
  78.6 0.7 shard_map.33
  79.3 0.0 collective-permute-done.1.theirs_ref
  79.3 15.0 %shard_map.34 = f32[384,256]{1,0:T(8,128)} custom-call(s32[2]{0:T(128)S(1)} %pad_add_fusion.core_ref.place_ref, f32[16,9,4,128]{3,2,1,0:T(4,128)S(1)} %all-to-all-done.3.mine_ref, f32[16,9,4,128]{3,2,1,0:T(4,128)S(1)} %collective-permute-done.1.theirs_ref, bf16[4,384,128]{2,1,0:T(8,128)(2,1)S(1)} %get-tuple-element.12.high_ref, ...), custom_call_target="tpu_custom_call" | custom-call | tf_op jit(solution)/shard_map/pallas_call | solution.py:456
Async XLA Ops:
  42.4 1.9 %collective-permute-start = (f32[32,24,128]{2,1,0:T(8,128)S(1)}, f32[32,24,128]{2,1,0:T(8,128)S(1)}, u32[]{:S(2)}, u32[]{:S(2)}) collective-permute-start(f32[32,24,128]{2,1,0:T(8,128)S(1)} %all_to_all.21.in_ref), channel_id=1, source_target_pairs={{0,8},{8,0},{1,9},{9,1},{2,10},{10,2},{3,11},{11,3},{4,12},{12,4},... | collective-permute-start | bytes 1179656 | tf_op jit(solution)/shard_map/ppermute | solution.py:508
  61.6 13.9 %all-to-all-start.3 = ((f32[16,9,4,128]{3,2,1,0:T(4,128)}), f32[16,9,4,128]{3,2,1,0:T(4,128)S(1)}, u32[]{:S(2)}, u32[]{:S(2)}) async-start(f32[16,9,4,128]{3,2,1,0:T(4,128)} %shard_map.32), calls=%async_computation.3 | async-start | bytes 589824 | tf_op jit(solution)/shard_map/all_to_all | solution.py:532
  65.1 13.5 %collective-permute-start.2 = (f32[4,192,128]{2,1,0:T(8,128)S(1)}, f32[4,192,128]{2,1,0:T(8,128)S(1)}, u32[]{:S(2)}, u32[]{:S(2)}) collective-permute-start(f32[4,192,128]{2,1,0:T(8,128)S(1)} %get-tuple-element.11.own_ref), channel_id=1, source_target_pairs={{0,1},{1,0},{2,3},{3,2},{4,5},{5,4},{6,7},{7,6},{8,9},{9,8},{10,11... | collective-permute-start | bytes 1179656 | tf_op jit(solution)/shard_map/ppermute | solution.py:529
  75.5 3.9 %collective-permute-start.1 = (f32[16,9,4,128]{3,2,1,0:T(4,128)S(1)}, f32[16,9,4,128]{3,2,1,0:T(4,128)S(1)}, u32[]{:S(2)}, u32[]{:S(2)}) collective-permute-start(f32[16,9,4,128]{3,2,1,0:T(4,128)S(1)} %all-to-all-done.3.mine_ref), channel_id=1, source_target_pairs={{0,8},{8,0},{1,9},{9,1},{2,10},{10,2},{3,11},{11,3},{4,12},{12,4},... | collective-permute-start | bytes 884744 | tf_op jit(solution)/shard_map/ppermute | solution.py:533

commit v3 on v1

--- a/solution.py
+++ b/solution.py
@@ -1,4 +1,5 @@
 import functools
+import math
 
 import jax
 import jax.numpy as jnp
@@ -179,24 +180,28 @@
         along_y = jnp.where(lane // total_y == part, value.astype(jnp.float32), along_y)
     along_y = along_y.astype(jnp.bfloat16)
 
+    together = math.gcd(total_x, 4)
     for step in range(DEGREE):
         now, other = step % 2, (step + 1) % 2
         scale = 1.0 / half_width if step == 0 else 2.0 / half_width
         for x in range(total_x):
             value = field[now, WIDTH + x]
-            parts = split(value)
-            lap = lax.dot_general(
-                jnp.concatenate(left_parts(parts), axis=1),
-                along_z,
-                (((1,), (0,)), ((), ())),
-                preferred_element_type=jnp.float32,
-            )
-            lap = lap + lax.dot_general(
-                along_y,
-                jnp.concatenate(right_parts(parts), axis=0),
-                (((1,), (0,)), ((), ())),
-                preferred_element_type=jnp.float32,
-            )
+            if x % together == 0:
+                parts = [split(field[now, WIDTH + near]) for near in range(x, x + together)]
+                sum_z = lax.dot_general(
+                    jnp.concatenate([jnp.concatenate(left_parts(part), axis=1) for part in parts], axis=0),
+                    along_z,
+                    (((1,), (0,)), ((), ())),
+                    preferred_element_type=jnp.float32,
+                )
+                sum_y = lax.dot_general(
+                    along_y,
+                    jnp.concatenate([jnp.concatenate(right_parts(part), axis=0) for part in parts], axis=1),
+                    (((1,), (0,)), ((), ())),
+                    preferred_element_type=jnp.float32,
+                )
+            n = x % together
+            lap = sum_z[total_y * n : total_y * (n + 1)] + sum_y[:, LANES * n : LANES * (n + 1)]
             for k in range(1, WIDTH + 1):
                 lap = lap + coeffs[k] * (field[now, WIDTH + x + k] + field[now, WIDTH + x - k])
             result = (potential[x] * value - 0.5 * lap) * scale

time: 93.8 us -> 92.7 us (0.988)
  Pallas kernels: 24.1 us -> 23 us
    pallas_call x5, Pallas kernels: 21.7 us -> 20.6 us  [call(): pl.pallas_call(kernel, out_shape=jax.ShapeDtypeStruct(shape, jnp.float32)...]
where the time goes in v3:
time: 92.7 us; the launch traced here: 92.4 us
  blocking collectives  51.6 us (56%)
  Pallas kernels  23 us (25%)
  waiting for transfers between devices  12.4 us (13%)
  starting transfers between devices  5.35 us (6%)
    all_to_all x1, blocking collectives, transposed(): packed = lax.all_to_all(packed, area, 0, 0, tiled=True)  20.7 us
    pallas_call x5, Pallas kernels, call(): pl.pallas_call(kernel, out_shape=jax.ShapeDtypeStruct(shape, jnp.float32)...  20.6 us
    all_to_all x1, blocking collectives, transposed(): filtered = lax.all_to_all(filtered, everyone, 0, 0, tiled=True)  16.6 us
    all_to_all x1, blocking collectives, transposed(): lax.all_to_all(partial.reshape(holders, rows // holders // TILE, TILE, LA...  14.3 us
    all_to_all x1, waiting for transfers between devices, transposed(): mine = lax.all_to_all(pieces, same_core, 0, 0, tiled=True)  8.17 us
    all_to_all x1, starting transfers between devices, transposed(): mine = lax.all_to_all(pieces, same_core, 0, 0, tiled=True)  3.54 us
    ppermute x1, waiting for transfers between devices, transposed(): other = lax.ppermute(own, 'band', swap)  3.15 us
  transfers between devices with their start and end apart: 4, of which 3 were waited for; matrix products, arithmetic and copies ran while one was open for 0% of the time, Pallas kernels for 1%

profile of v3, /device:TPU:0, one launch (start us, length us, event | category | flops | bytes accessed | tf_op | source)
XLA Modules:
  0.0 92.4 jit_solution(18320952349437995737)
XLA Ops:
  0.0 1.7 %shard_map.28 = f32[16,13,4,128]{3,2,1,0:T(4,128)S(1)} custom-call(f32[384,256]{1,0:T(8,128)} %bitcast.6, f32[6,8,8]{2,1,0:T(8,128)} %potential_in.1), custom_call_target="tpu_custom_call" | custom-call | tf_op jit(solution)/shard_map/pallas_call | solution.py:468
  1.7 20.7 %all_to_all.20.in_ref = f32[16,13,4,128]{3,2,1,0:T(4,128)S(1)} all-to-all(f32[16,13,4,128]{3,2,1,0:T(4,128)S(1)} %shard_map.28), channel_id=1, replica_groups=mesh['chip'=2,'core'=2,'dy'=4,'band'=2] {'chip','core','dy'}, dimensions={0} | all-to-all | bytes 851968 | tf_op jit(solution)/shard_map/all_to_all | solution.py:480
  22.3 2.4 %shard_map.29 = f32[32,24,128]{2,1,0:T(8,128)S(1)} custom-call(f32[16,13,4,128]{3,2,1,0:T(4,128)S(1)} %all_to_all.20.in_ref), custom_call_target="tpu_custom_call" | custom-call | tf_op jit(solution)/shard_map/pallas_call | solution.py:444
  24.7 16.6 %all_to_all.21.in_ref = f32[32,24,128]{2,1,0:T(8,128)S(1)} all-to-all(f32[32,24,128]{2,1,0:T(8,128)S(1)} %shard_map.29), channel_id=1, replica_groups=mesh['chip'=2,'core'=2,'dy'=4,'band'=2] {'chip','core','dy','band'}, dimensions={0} | all-to-all | bytes 786432 | tf_op jit(solution)/shard_map/all_to_all | solution.py:491
  41.3 0.0 collective-permute-start
  41.3 0.1 pad_add_fusion.core_ref.place_ref
  41.4 0.6 shard_map.30.own_ref
  42.0 1.0 %collective-permute-done.other_in = f32[32,24,128]{2,1,0:T(8,128)S(1)} collective-permute-done((f32[32,24,128]{2,1,0:T(8,128)S(1)}, f32[32,24,128]{2,1,0:T(8,128)S(1)}, u32[]{:S(2)}, u32[]{:S(2)}) %collective-permute-start) | collective-permute-done | bytes 393248 | tf_op jit(solution)/shard_map/ppermute | solution.py:496
  43.0 1.9 %shard_map.31 = f32[144,4,128]{2,1,0:T(4,128)S(1)} custom-call(s32[2]{0:T(128)S(1)} %pad_add_fusion.core_ref.place_ref, f32[4,192,128]{2,1,0:T(8,128)S(1)} %shard_map.30.own_ref, f32[32,24,128]{2,1,0:T(8,128)S(1)} %collective-permute-done.other_in), custom_call_target="tpu_custom_call" | custom-call | tf_op jit(solution)/shard_map/pallas_call | solution.py:444
  44.9 14.3 %all_to_all.22.in_ref = f32[16,9,4,128]{3,2,1,0:T(4,128)S(1)} all-to-all(f32[16,9,4,128]{3,2,1,0:T(4,128)S(1)} %bitcast.5), channel_id=1, replica_groups=mesh['chip'=2,'core'=2,'dy'=4,'band'=2] {'chip','dy','band'}, dimensions={0} | all-to-all | bytes 589824 | tf_op jit(solution)/shard_map/all_to_all | solution.py:509
  59.2 0.8 shard_map.32
  60.0 3.5 %all-to-all-start.3 = ((f32[16,9,4,128]{3,2,1,0:T(4,128)}), f32[16,9,4,128]{3,2,1,0:T(4,128)S(1)}, u32[]{:S(2)}, u32[]{:S(2)}) async-start(f32[16,9,4,128]{3,2,1,0:T(4,128)} %shard_map.32), calls=%async_computation.3 | async-start | bytes 589824 | tf_op jit(solution)/shard_map/all_to_all | solution.py:511
  63.6 1.8 %collective-permute-start.2 = (f32[4,192,128]{2,1,0:T(8,128)S(1)}, f32[4,192,128]{2,1,0:T(8,128)S(1)}, u32[]{:S(2)}, u32[]{:S(2)}) collective-permute-start(f32[4,192,128]{2,1,0:T(8,128)S(1)} %shard_map.30.own_ref), channel_id=1, source_target_pairs={{0,1},{1,0},{2,3},{3,2},{4,5},{5,4},{6,7},{7,6},{8,9},{9,8},{10,11... | collective-permute-start | bytes 1179656 | tf_op jit(solution)/shard_map/ppermute | solution.py:508
  65.4 8.2 %all-to-all-done.3.mine_ref = f32[16,9,4,128]{3,2,1,0:T(4,128)S(1)} async-done(((f32[16,9,4,128]{3,2,1,0:T(4,128)}), f32[16,9,4,128]{3,2,1,0:T(4,128)S(1)}, u32[]{:S(2)}, u32[]{:S(2)}) %all-to-all-start.3) | async-done | bytes 294944 | tf_op jit(solution)/shard_map/all_to_all | solution.py:511
  73.5 0.0 collective-permute-start.1
  73.5 3.2 %collective-permute-done.2.other_ref = f32[4,192,128]{2,1,0:T(8,128)S(1)} collective-permute-done((f32[4,192,128]{2,1,0:T(8,128)S(1)}, f32[4,192,128]{2,1,0:T(8,128)S(1)}, u32[]{:S(2)}, u32[]{:S(2)}) %collective-permute-start.2) | collective-permute-done | bytes 393248 | tf_op jit(solution)/shard_map/ppermute | solution.py:508
  76.7 0.7 shard_map.33
  77.4 0.0 collective-permute-done.1.theirs_ref
  77.4 15.0 %shard_map.34 = f32[384,256]{1,0:T(8,128)} custom-call(s32[2]{0:T(128)S(1)} %pad_add_fusion.core_ref.place_ref, f32[16,9,4,128]{3,2,1,0:T(4,128)S(1)} %all-to-all-done.3.mine_ref, f32[16,9,4,128]{3,2,1,0:T(4,128)S(1)} %collective-permute-done.1.theirs_ref, bf16[4,384,128]{2,1,0:T(8,128)(2,1)S(1)} %get-tuple-element.8.high_ref, ...), custom_call_target="tpu_custom_call" | custom-call | tf_op jit(solution)/shard_map/pallas_call | solution.py:444
Async XLA Ops:
  41.3 1.7 %collective-permute-start = (f32[32,24,128]{2,1,0:T(8,128)S(1)}, f32[32,24,128]{2,1,0:T(8,128)S(1)}, u32[]{:S(2)}, u32[]{:S(2)}) collective-permute-start(f32[32,24,128]{2,1,0:T(8,128)S(1)} %all_to_all.21.in_ref), channel_id=1, source_target_pairs={{0,8},{8,0},{1,9},{9,1},{2,10},{10,2},{3,11},{11,3},{4,12},{12,4},... | collective-permute-start | bytes 1179656 | tf_op jit(solution)/shard_map/ppermute | solution.py:496
  60.0 13.5 %all-to-all-start.3 = ((f32[16,9,4,128]{3,2,1,0:T(4,128)}), f32[16,9,4,128]{3,2,1,0:T(4,128)S(1)}, u32[]{:S(2)}, u32[]{:S(2)}) async-start(f32[16,9,4,128]{3,2,1,0:T(4,128)} %shard_map.32), calls=%async_computation.3 | async-start | bytes 589824 | tf_op jit(solution)/shard_map/all_to_all | solution.py:511
  63.6 13.1 %collective-permute-start.2 = (f32[4,192,128]{2,1,0:T(8,128)S(1)}, f32[4,192,128]{2,1,0:T(8,128)S(1)}, u32[]{:S(2)}, u32[]{:S(2)}) collective-permute-start(f32[4,192,128]{2,1,0:T(8,128)S(1)} %shard_map.30.own_ref), channel_id=1, source_target_pairs={{0,1},{1,0},{2,3},{3,2},{4,5},{5,4},{6,7},{7,6},{8,9},{9,8},{10,11... | collective-permute-start | bytes 1179656 | tf_op jit(solution)/shard_map/ppermute | solution.py:508
  73.5 3.9 %collective-permute-start.1 = (f32[16,9,4,128]{3,2,1,0:T(4,128)S(1)}, f32[16,9,4,128]{3,2,1,0:T(4,128)S(1)}, u32[]{:S(2)}, u32[]{:S(2)}) collective-permute-start(f32[16,9,4,128]{3,2,1,0:T(4,128)S(1)} %all-to-all-done.3.mine_ref), channel_id=1, source_target_pairs={{0,8},{8,0},{1,9},{9,1},{2,10},{10,2},{3,11},{11,3},{4,12},{12,4},... | collective-permute-start | bytes 884744 | tf_op jit(solution)/shard_map/ppermute | solution.py:512

commit v4 on v3

--- a/solution.py
+++ b/solution.py
@@ -102,13 +102,12 @@
     lane = lax.broadcasted_iota(jnp.int32, (nz, LANES), 1)
     tiles = columns // TILE
     last.wait()
-    packed = jnp.zeros((TILE, LANES), jnp.float32)
-    for part in range(2):
-        wide = jnp.zeros((potential.shape[1], LANES), jnp.float32)
-        for x in range(potential.shape[0]):
-            spread = jnp.where(lane == row + nz * x + LANES // 2 * part, 1.0, 0.0)
-            wide = wide + dot(potential[x], spread, ((1,), (0,)))
-        packed = packed + wide[TILE * part : TILE * (part + 1)]
+    size_x, size_y, _ = potential.shape
+    wide = dot(potential[...].reshape(size_x * size_y, nz), jnp.where(lane % nz == row, 1.0, 0.0), ((1,), (0,)))
+    packed = jnp.zeros((size_y, LANES), jnp.float32)
+    for x in range(size_x):
+        packed = jnp.where(lane % (LANES // 2) // nz == x, wide[size_y * x : size_y * (x + 1)], packed)
+    packed = jnp.where(lane[:TILE] < LANES // 2, packed[:TILE], packed[TILE:])
     for i in range(out_ref.shape[0]):
         out_ref[i, tiles] = packed
     for half in halves:

time: 92.7 us -> 92.6 us (level)
  no operation moved by 1% of the time
where the time goes in v4:
time: 92.6 us; the launch traced here: 92.3 us
  blocking collectives  51.6 us (56%)
  Pallas kernels  22.8 us (25%)
  waiting for transfers between devices  12.4 us (13%)
  starting transfers between devices  5.35 us (6%)
    all_to_all x1, blocking collectives, transposed(): packed = lax.all_to_all(packed, area, 0, 0, tiled=True)  20.7 us
    pallas_call x5, Pallas kernels, call(): pl.pallas_call(kernel, out_shape=jax.ShapeDtypeStruct(shape, jnp.float32)...  20.6 us
    all_to_all x1, blocking collectives, transposed(): filtered = lax.all_to_all(filtered, everyone, 0, 0, tiled=True)  16.6 us
    all_to_all x1, blocking collectives, transposed(): lax.all_to_all(partial.reshape(holders, rows // holders // TILE, TILE, LA...  14.3 us
    all_to_all x1, waiting for transfers between devices, transposed(): mine = lax.all_to_all(pieces, same_core, 0, 0, tiled=True)  8.17 us
    all_to_all x1, starting transfers between devices, transposed(): mine = lax.all_to_all(pieces, same_core, 0, 0, tiled=True)  3.54 us
    ppermute x1, waiting for transfers between devices, transposed(): other = lax.ppermute(own, 'band', swap)  3.15 us
  transfers between devices with their start and end apart: 4, of which 3 were waited for; matrix products, arithmetic and copies ran while one was open for 0% of the time, Pallas kernels for 1%

profile of v4, /device:TPU:0, one launch (start us, length us, event | category | flops | bytes accessed | tf_op | source)
XLA Modules:
  0.0 92.3 jit_solution(12857397387018064984)
XLA Ops:
  0.0 1.6 %shard_map.28 = f32[16,13,4,128]{3,2,1,0:T(4,128)S(1)} custom-call(f32[384,256]{1,0:T(8,128)} %bitcast.6, f32[6,8,8]{2,1,0:T(8,128)} %potential_in.1), custom_call_target="tpu_custom_call" | custom-call | tf_op jit(solution)/shard_map/pallas_call | solution.py:467
  1.6 20.7 %all_to_all.20.in_ref = f32[16,13,4,128]{3,2,1,0:T(4,128)S(1)} all-to-all(f32[16,13,4,128]{3,2,1,0:T(4,128)S(1)} %shard_map.28), channel_id=1, replica_groups=mesh['chip'=2,'core'=2,'dy'=4,'band'=2] {'chip','core','dy'}, dimensions={0} | all-to-all | bytes 851968 | tf_op jit(solution)/shard_map/all_to_all | solution.py:479
  22.2 2.4 %shard_map.29 = f32[32,24,128]{2,1,0:T(8,128)S(1)} custom-call(f32[16,13,4,128]{3,2,1,0:T(4,128)S(1)} %all_to_all.20.in_ref), custom_call_target="tpu_custom_call" | custom-call | tf_op jit(solution)/shard_map/pallas_call | solution.py:443
  24.6 16.6 %all_to_all.21.in_ref = f32[32,24,128]{2,1,0:T(8,128)S(1)} all-to-all(f32[32,24,128]{2,1,0:T(8,128)S(1)} %shard_map.29), channel_id=1, replica_groups=mesh['chip'=2,'core'=2,'dy'=4,'band'=2] {'chip','core','dy','band'}, dimensions={0} | all-to-all | bytes 786432 | tf_op jit(solution)/shard_map/all_to_all | solution.py:490
  41.2 0.0 collective-permute-start
  41.2 0.1 pad_add_fusion.core_ref.place_ref
  41.3 0.6 shard_map.30.own_ref
  41.9 1.0 %collective-permute-done.other_in = f32[32,24,128]{2,1,0:T(8,128)S(1)} collective-permute-done((f32[32,24,128]{2,1,0:T(8,128)S(1)}, f32[32,24,128]{2,1,0:T(8,128)S(1)}, u32[]{:S(2)}, u32[]{:S(2)}) %collective-permute-start) | collective-permute-done | bytes 393248 | tf_op jit(solution)/shard_map/ppermute | solution.py:495
  42.9 1.9 %shard_map.31 = f32[144,4,128]{2,1,0:T(4,128)S(1)} custom-call(s32[2]{0:T(128)S(1)} %pad_add_fusion.core_ref.place_ref, f32[4,192,128]{2,1,0:T(8,128)S(1)} %shard_map.30.own_ref, f32[32,24,128]{2,1,0:T(8,128)S(1)} %collective-permute-done.other_in), custom_call_target="tpu_custom_call" | custom-call | tf_op jit(solution)/shard_map/pallas_call | solution.py:443
  44.8 14.3 %all_to_all.22.in_ref = f32[16,9,4,128]{3,2,1,0:T(4,128)S(1)} all-to-all(f32[16,9,4,128]{3,2,1,0:T(4,128)S(1)} %bitcast.5), channel_id=1, replica_groups=mesh['chip'=2,'core'=2,'dy'=4,'band'=2] {'chip','dy','band'}, dimensions={0} | all-to-all | bytes 589824 | tf_op jit(solution)/shard_map/all_to_all | solution.py:508
  59.1 0.8 shard_map.32
  59.9 3.5 %all-to-all-start.3 = ((f32[16,9,4,128]{3,2,1,0:T(4,128)}), f32[16,9,4,128]{3,2,1,0:T(4,128)S(1)}, u32[]{:S(2)}, u32[]{:S(2)}) async-start(f32[16,9,4,128]{3,2,1,0:T(4,128)} %shard_map.32), calls=%async_computation.3 | async-start | bytes 589824 | tf_op jit(solution)/shard_map/all_to_all | solution.py:510
  63.4 1.8 %collective-permute-start.2 = (f32[4,192,128]{2,1,0:T(8,128)S(1)}, f32[4,192,128]{2,1,0:T(8,128)S(1)}, u32[]{:S(2)}, u32[]{:S(2)}) collective-permute-start(f32[4,192,128]{2,1,0:T(8,128)S(1)} %shard_map.30.own_ref), channel_id=1, source_target_pairs={{0,1},{1,0},{2,3},{3,2},{4,5},{5,4},{6,7},{7,6},{8,9},{9,8},{10,11... | collective-permute-start | bytes 1179656 | tf_op jit(solution)/shard_map/ppermute | solution.py:507
  65.2 8.2 %all-to-all-done.3.mine_ref = f32[16,9,4,128]{3,2,1,0:T(4,128)S(1)} async-done(((f32[16,9,4,128]{3,2,1,0:T(4,128)}), f32[16,9,4,128]{3,2,1,0:T(4,128)S(1)}, u32[]{:S(2)}, u32[]{:S(2)}) %all-to-all-start.3) | async-done | bytes 294944 | tf_op jit(solution)/shard_map/all_to_all | solution.py:510
  73.4 0.0 collective-permute-start.1
  73.4 3.2 %collective-permute-done.2.other_ref = f32[4,192,128]{2,1,0:T(8,128)S(1)} collective-permute-done((f32[4,192,128]{2,1,0:T(8,128)S(1)}, f32[4,192,128]{2,1,0:T(8,128)S(1)}, u32[]{:S(2)}, u32[]{:S(2)}) %collective-permute-start.2) | collective-permute-done | bytes 393248 | tf_op jit(solution)/shard_map/ppermute | solution.py:507
  76.6 0.7 shard_map.33
  77.3 0.0 collective-permute-done.1.theirs_ref
  77.3 15.0 %shard_map.34 = f32[384,256]{1,0:T(8,128)} custom-call(s32[2]{0:T(128)S(1)} %pad_add_fusion.core_ref.place_ref, f32[16,9,4,128]{3,2,1,0:T(4,128)S(1)} %all-to-all-done.3.mine_ref, f32[16,9,4,128]{3,2,1,0:T(4,128)S(1)} %collective-permute-done.1.theirs_ref, bf16[4,384,128]{2,1,0:T(8,128)(2,1)S(1)} %get-tuple-element.8.high_ref, ...), custom_call_target="tpu_custom_call" | custom-call | tf_op jit(solution)/shard_map/pallas_call | solution.py:443
Async XLA Ops:
  41.2 1.7 %collective-permute-start = (f32[32,24,128]{2,1,0:T(8,128)S(1)}, f32[32,24,128]{2,1,0:T(8,128)S(1)}, u32[]{:S(2)}, u32[]{:S(2)}) collective-permute-start(f32[32,24,128]{2,1,0:T(8,128)S(1)} %all_to_all.21.in_ref), channel_id=1, source_target_pairs={{0,8},{8,0},{1,9},{9,1},{2,10},{10,2},{3,11},{11,3},{4,12},{12,4},... | collective-permute-start | bytes 1179656 | tf_op jit(solution)/shard_map/ppermute | solution.py:495
  59.9 13.5 %all-to-all-start.3 = ((f32[16,9,4,128]{3,2,1,0:T(4,128)}), f32[16,9,4,128]{3,2,1,0:T(4,128)S(1)}, u32[]{:S(2)}, u32[]{:S(2)}) async-start(f32[16,9,4,128]{3,2,1,0:T(4,128)} %shard_map.32), calls=%async_computation.3 | async-start | bytes 589824 | tf_op jit(solution)/shard_map/all_to_all | solution.py:510
  63.4 13.1 %collective-permute-start.2 = (f32[4,192,128]{2,1,0:T(8,128)S(1)}, f32[4,192,128]{2,1,0:T(8,128)S(1)}, u32[]{:S(2)}, u32[]{:S(2)}) collective-permute-start(f32[4,192,128]{2,1,0:T(8,128)S(1)} %shard_map.30.own_ref), channel_id=1, source_target_pairs={{0,1},{1,0},{2,3},{3,2},{4,5},{5,4},{6,7},{7,6},{8,9},{9,8},{10,11... | collective-permute-start | bytes 1179656 | tf_op jit(solution)/shard_map/ppermute | solution.py:507
  73.4 3.9 %collective-permute-start.1 = (f32[16,9,4,128]{3,2,1,0:T(4,128)S(1)}, f32[16,9,4,128]{3,2,1,0:T(4,128)S(1)}, u32[]{:S(2)}, u32[]{:S(2)}) collective-permute-start(f32[16,9,4,128]{3,2,1,0:T(4,128)S(1)} %all-to-all-done.3.mine_ref), channel_id=1, source_target_pairs={{0,8},{8,0},{1,9},{9,1},{2,10},{10,2},{3,11},{11,3},{4,12},{12,4},... | collective-permute-start | bytes 884744 | tf_op jit(solution)/shard_map/ppermute | solution.py:511
